TPU v7x, 32 devices: a whole 2x2x4 slice. The times are simulated.
32 devices in a mesh: group: 2 (over x), seq: 16 (over z, y, core).
Axes of the slice: x: 2, y: 2, z: 4, core: 2. Of those that a mesh axis runs over, the one named last changes fastest.
Arguments:
- queries: bfloat16 [8192, 768], P(('group', 'seq')), parts along dimension 0, may hold values from -6 to 6
- key_rows: bfloat16 [8192, 768], P(('group', 'seq')), parts along dimension 0, may hold values from -6 to 6
- value_rows: bfloat16 [8192, 768], P(('group', 'seq')), parts along dimension 0, may hold values from -20 to 20
- dilation: int32 [12], replicated, may hold values from 2 to 30, as said below
- global_rows: int32 [128], P('group'), parts along dimension 0, may hold values from 0 to 4095, as said below
- out_weight: bfloat16 [768, 1536], replicated, may hold values from -0.21875 to 0.21875
- mlp_up: bfloat16 [1536, 3072], P('seq'), may hold values from -0.15625 to 0.15625
- mlp_down: bfloat16 [3072, 1536], P('seq'), may hold values from -0.109375 to 0.109375
Outputs:
- attended: bfloat16 [8192, 1536], P(('group', 'seq')), parts along dimension 0
- mlp_out: bfloat16 [8192, 1536], P(('group', 'seq')), parts along dimension 0
There are 2 independent parts, one for each index of `group`. A program takes and returns all parts, laid end to end along the dimension named above; an argument that names none is the same for every part. Nothing has to cross between parts.
Inputs may be any that keep to these rules, and one draw needn't show every extreme that they name: `dilation`: each offset is a multiple of 2; some head has the smallest and some the largest. `global_rows`: distinct positions.
All inputs are finite; a program needn't handle non-finite values.
Results may differ from a plain program's by a relative error of at most 0.0071.
Values may be sent and summed in bfloat16 or wider, within the bound.
A program may use at most 192 MiB of HBM per device.

v0:
```python
import jax
import jax.numpy as jnp
from jax import lax
from jax.sharding import PartitionSpec as P

H = 12
DH = 64
BLK = 128
GLOBALS = 64


def with_halo(cells, sides, width):
    for axis, dim in sides:
        count = lax.axis_size(axis)
        head = lax.slice_in_dim(cells, 0, width, axis=dim)
        tail = lax.slice_in_dim(cells, cells.shape[dim] - width, cells.shape[dim], axis=dim)
        cells = jnp.concatenate(
            [
                lax.ppermute(tail, axis, [(i, (i + 1) % count) for i in range(count)]),
                cells,
                lax.ppermute(head, axis, [((i + 1) % count, i) for i in range(count)]),
            ],
            axis=dim,
        )
    return cells


def passed_along(value, axis, steps):
    count = lax.axis_size(axis)
    pairs = [(source, (source + steps) % count) for source in range(count)]
    return lax.ppermute(value, axis, pairs)


def merged_2(part, axis, combine):
    gathered = jax.tree.map(lambda a: lax.all_gather(a, axis), part)

    def take(source):
        return jax.tree.map(lambda a: lax.dynamic_index_in_dim(a, source, 0, False), gathered)

    return lax.fori_loop(
        1, lax.axis_size(axis), lambda source, state: combine(state, take(source)), take(0)
    )


def attend_blocks(query_blocks, local_keys, local_values, glob_keys, glob_values):
    count = query_blocks.shape[0]
    keys_all = jnp.concatenate(
        [local_keys, jnp.broadcast_to(glob_keys[None], (count,) + glob_keys.shape)], axis=1
    )
    values_all = jnp.concatenate(
        [local_values, jnp.broadcast_to(glob_values[None], (count,) + glob_values.shape)], axis=1
    )
    scores = jnp.einsum(
        "nqhd,nkhd->nhqk", query_blocks, keys_all, preferred_element_type=jnp.float32
    ) * DH ** (-0.5)
    peak = jnp.max(scores, axis=-1, keepdims=True)
    exp_terms = jnp.exp(scores - peak)
    totals = jnp.sum(exp_terms, axis=-1, keepdims=True)
    weights = (exp_terms / totals).astype(jnp.bfloat16)
    return jnp.einsum("nhqk,nkhd->nqhd", weights, values_all, preferred_element_type=jnp.float32)


def select_heads(chosen, arrived, current):
    shaped = current.shape
    head_mask = chosen[None, None, :, None]
    merged = jnp.where(
        head_mask,
        arrived.reshape(shaped[0], shaped[1], H, DH),
        current.reshape(shaped[0], shaped[1], H, DH),
    )
    return merged.reshape(shaped)


def join_partials(first, second):
    peak_first, total_first, numer_first = first
    peak_second, total_second, numer_second = second
    highest = jnp.maximum(peak_first, peak_second)
    scale_first = jnp.exp(peak_first - highest)
    scale_second = jnp.exp(peak_second - highest)
    return (
        highest,
        total_first * scale_first + total_second * scale_second,
        numer_first * scale_first[:, :, None] + numer_second * scale_second[:, :, None],
    )


def per_device(queries, key_rows, value_rows, dilation, global_rows, out_weight, mlp_up, mlp_down):
    tok_rows = queries.shape[0]
    blocks = tok_rows // BLK
    devices = lax.axis_size("seq")
    stacked = jnp.stack([key_rows, value_rows])
    padded = with_halo(stacked, (("seq", 1),), BLK)
    dev_hops = dilation // blocks
    current = stacked
    for bit_level in range((devices - 1).bit_length()):
        arrived = passed_along(current, "seq", -(1 << bit_level))
        chosen = dev_hops >> bit_level & 1 == 1
        current = select_heads(chosen, arrived, current)
    start = lax.axis_index("seq") * tok_rows
    offsets = global_rows - start
    onehot = offsets[:, None] == jnp.arange(tok_rows, dtype=jnp.int32)[None, :]
    picker = onehot.astype(jnp.bfloat16)
    picked = (
        jnp.dot(picker, queries, preferred_element_type=jnp.float32),
        jnp.dot(picker, key_rows, preferred_element_type=jnp.float32),
        jnp.dot(picker, value_rows, preferred_element_type=jnp.float32),
    )
    glob_q, glob_k, glob_v = lax.psum((picked[0], picked[1], picked[2]), "seq")
    glob_query = glob_q.astype(jnp.bfloat16).reshape(GLOBALS, H, DH)
    glob_keys = glob_k.astype(jnp.bfloat16).reshape(GLOBALS, H, DH)
    glob_values = glob_v.astype(jnp.bfloat16).reshape(GLOBALS, H, DH)
    grid = padded.reshape(2, blocks + 2, BLK, H, DH)
    dilated = current.reshape(2, blocks, BLK, H, DH)
    local_set = jnp.concatenate([grid[:, :-2], grid[:, 1:-1], grid[:, 2:], dilated], axis=2)
    attended_local = attend_blocks(
        queries.reshape(blocks, BLK, H, DH), local_set[0], local_set[1], glob_keys, glob_values
    ).reshape(tok_rows, H * DH)
    scores = jnp.einsum(
        "ghd,thd->hgt",
        glob_query,
        key_rows.reshape(tok_rows, H, DH),
        preferred_element_type=jnp.float32,
    ) * DH ** (-0.5)
    peak = jnp.max(scores, axis=2)
    exp_terms = jnp.exp(scores - peak[:, :, None])
    totals = jnp.sum(exp_terms, axis=2)
    numerators = jnp.einsum(
        "hgt,thd->hgd",
        exp_terms,
        value_rows.astype(jnp.float32).reshape(tok_rows, H, DH),
        precision=lax.Precision.HIGHEST,
    )
    peak, totals, numerators = merged_2((peak, totals, numerators), "seq", join_partials)
    glob_out = (numerators / totals[:, :, None]).transpose(1, 0, 2).reshape(GLOBALS, H * DH)
    onehot_float = onehot.astype(jnp.float32)
    placed = jnp.dot(onehot_float.T, glob_out, precision=lax.Precision.HIGHEST)
    owned_rows = jnp.sum(onehot_float, axis=0) > 0.5
    attention = jnp.where(owned_rows[:, None], placed, attended_local).astype(jnp.bfloat16)
    attended = jnp.dot(attention, out_weight, preferred_element_type=jnp.float32).astype(
        jnp.bfloat16
    )
    columns = attended
    pre_act = jnp.dot(
        columns,
        lax.all_gather(mlp_up, "seq", axis=0, tiled=True),
        preferred_element_type=jnp.float32,
    )
    hidden = jax.nn.gelu(pre_act, approximate=True).astype(jnp.bfloat16)
    columns = hidden
    mlp_out = jnp.dot(
        columns,
        lax.all_gather(mlp_down, "seq", axis=0, tiled=True),
        preferred_element_type=jnp.float32,
    ).astype(jnp.bfloat16)
    return (attended, mlp_out)


def solution(mesh):
    placed = (
        P(("group", "seq"), None),
        P(("group", "seq"), None),
        P(("group", "seq"), None),
        P(),
        P("group"),
        P(),
        P("seq", None),
        P("seq", None),
    )
    return jax.shard_map(
        per_device,
        mesh=mesh,
        in_specs=placed,
        out_specs=(P(("group", "seq"), None), P(("group", "seq"), None)),
        check_vma=False,
    )
```

profile of v0, /device:TPU:0, one launch (start us, length us, event | category | flops | bytes accessed | tf_op | source)
XLA Modules:
  0.0 397.6 jit_solution(10071234965016458596)
XLA Ops:
  13.0 2.0 copy.69
  15.0 2.0 fusion.49
  17.0 70.1 %all-reduce.2 = (bf16[64,768]{1,0:T(8,128)(2,1)}, bf16[64,768]{1,0:T(8,128)(2,1)}, bf16[64,768]{1,0:T(8,128)(2,1)}) all-reduce(f32[64,768]{1,0:T(8,128)} %fusion.47, f32[64,768]{1,0:T(8,128)} %fusion.48, f32[64,768]{1,0:T(8,128)} %fusion.49), channel_id=1, replica_groups=mesh['group'=2,'seq'=16] {'seq'}, use_global_device_ids=true, to_apply=%region_7.8 | all-reduce | flops 147456 | bytes 884736 | tf_op jit(solution)/shard_map/psum | solution.py:108
  91.1 2.4 fusion.37
  97.8 19.8 %collective-permute-done.2 = bf16[2,256,768]{2,1,0:T(8,128)(2,1)} collective-permute-done((bf16[2,256,768]{2,1,0:T(8,128)(2,1)}, bf16[2,256,768]{2,1,0:T(8,128)(2,1)}, u32[]{:S(2)}, u32[]{:S(2)}) %collective-permute-start.2) | collective-permute-done | bytes 786464 | tf_op jit(solution)/shard_map/ppermute | solution.py:31
  117.6 2.1 broadcast_select_fusion
  121.1 17.6 %collective-permute-done.3 = bf16[2,256,768]{2,1,0:T(8,128)(2,1)} collective-permute-done((bf16[2,256,768]{2,1,0:T(8,128)(2,1)}, bf16[2,256,768]{2,1,0:T(8,128)(2,1)}, u32[]{:S(2)}, u32[]{:S(2)}) %collective-permute-start.3) | collective-permute-done | bytes 786464 | tf_op jit(solution)/shard_map/ppermute | solution.py:31
  138.8 2.4 broadcast_select_fusion.1
  142.1 15.3 %collective-permute-start = (bf16[2,128,768]{2,1,0:T(8,128)(2,1)}, bf16[2,128,768]{2,1,0:T(8,128)(2,1)}, u32[]{:S(2)}, u32[]{:S(2)}) collective-permute-start(bf16[2,128,768]{2,1,0:T(8,128)(2,1)} %get-tuple-element.209), channel_id=1, source_target_pairs={{0,1},{1,2},{2,3},{3,4},{4,5},{5,6},{6,7},{7,8},{8,9},{9,10},{10,1... | collective-permute-start | bytes 1179656 | tf_op jit(solution)/shard_map/ppermute | solution.py:19
  157.4 4.5 %collective-permute-start.1 = (bf16[2,128,768]{2,1,0:T(8,128)(2,1)}, bf16[2,128,768]{2,1,0:T(8,128)(2,1)}, u32[]{:S(2)}, u32[]{:S(2)}) collective-permute-start(bf16[2,128,768]{2,1,0:T(8,128)(2,1)} %get-tuple-element.210), channel_id=1, source_target_pairs={{1,0},{2,1},{3,2},{4,3},{5,4},{6,5},{7,6},{8,7},{9,8},{10,9},{11,1... | collective-permute-start | bytes 1179656 | tf_op jit(solution)/shard_map/ppermute | solution.py:21
  176.9 23.6 %all-gather.4 = f32[16,12,64]{2,1,0:T(8,128)S(1)} all-gather(f32[1,12,64]{2,1,0:T(8,128)S(1)} %bitcast.103), channel_id=3, replica_groups=mesh['group'=2,'seq'=16] {'seq'}, dimensions={0}, use_global_device_ids=true | all-gather | bytes 52224 | tf_op jit(solution)/shard_map/all_gather | solution.py:35
  200.6 18.3 %all-gather.3 = f32[16,12,64]{2,1,0:T(8,128)S(1)} all-gather(f32[1,12,64]{2,1,0:T(8,128)S(1)} %bitcast.102), channel_id=2, replica_groups=mesh['group'=2,'seq'=16] {'seq'}, dimensions={0}, use_global_device_ids=true | all-gather | bytes 52224 | tf_op jit(solution)/shard_map/all_gather | solution.py:35
  219.5 2.4 broadcast_select_fusion.2
  222.5 2.4 pad_maximum_fusion.2
  224.9 2.6 copy.71
  227.5 3.5 reshape.91
  231.0 5.1 %fusion.65 = (bf16[2,2,128,12,64]{2,1,4,3,0:T(2,128)(2,1)S(1)}, bf16[2,2,128,12,64]{2,1,4,3,0:T(2,128)(2,1)S(1)}, bf16[2,2,128,12,64]{2,1,4,3,0:T(2,128)(2,1)S(1)}) fusion(bf16[2,4,128,12,64]{2,1,4,3,0:T(4,128)(2,1)} %reshape.91), kind=kLoop, calls=%fused_computation.98 | loop fusion | bytes 4718592 | tf_op jit(solution)/shard_map/slice | solution.py:114
  238.6 2.3 copy.78
  240.9 2.8 reshape.95
  243.7 2.3 copy.77
  246.0 2.7 reshape.94
  248.7 2.3 copy.76
  251.0 2.7 reshape.93
  253.7 39.6 %collective-permute-done.5 = bf16[2,256,768]{2,1,0:T(8,128)(2,1)} collective-permute-done((bf16[2,256,768]{2,1,0:T(8,128)(2,1)}, bf16[2,256,768]{2,1,0:T(8,128)(2,1)}, u32[]{:S(2)}, u32[]{:S(2)}) %collective-permute-start.5) | collective-permute-done | bytes 786464 | tf_op jit(solution)/shard_map/ppermute | solution.py:31
  293.3 2.3 copy.75
  295.6 2.7 reshape.92
  298.3 2.6 fusion.36
  303.6 7.2 %fusion.66 = (f32[2,12,128]{2,1,0:T(8,128)S(1)}, f32[2,12,128,576]{2,3,1,0:T(8,128)}) fusion(bf16[2,64,12,64]{1,3,2,0:T(8,128)(2,1)S(1)} %broadcast_in_dim.97, bf16[2,512,12,64]{1,3,2,0:T(8,128)(2,1)} %get-tuple-element.205, bf16[2,128,12,64]{1,0,3,2:T(2,128)(2,1)S(1)} %copy-done.8), kind=kOutput, calls=%fused_computation.99 | convolution fusion | flops 235340352 | bytes 9252864 | tf_op jit(solution)/shard_map/sub | solution.py:57
  310.9 4.3 %fusion.30 = bf16[2,128,12,64]{1,3,2,0:T(8,128)(2,1)S(1)} fusion(f32[2,12,128,576]{2,3,1,0:T(8,128)} %get-tuple-element.215, f32[2,12,128]{2,1,0:T(8,128)S(1)} %get-tuple-element.214, bf16[2,64,12,64]{1,3,2,0:T(8,128)(2,1)S(1)} %broadcast_in_dim.95, bf16[2,512,12,64]{1,3,2,0:T(8,128)(2,1)} %get-tuple-element.204), kind=kOutput, calls=%fused_computation.42 | convolution fusion | flops 233570304 | bytes 9252864 | tf_op jit(solution)/shard_map/nhqk,nkhd->nqhd/dot_general | solution.py:60
  317.0 32.2 %while.19 = (s32[]{:T(128)}, f32[12,64]{1,0:T(8,128)S(1)}, f32[12,64]{1,0:T(8,128)S(1)}, f32[12,64,64]{2,1,0:T(8,128)S(1)}, f32[16,12,64]{2,1,0:T(8,128)}, /*ind...) while((s32[]{:T(128)}, f32[12,64]{1,0:T(8,128)S(1)}, ...), condition=%wide.region_5.6_spmd, body=%wide.region_4.5_spmd.sunk | while | flops 152069 | bytes 620695 | solution.py:40
  351.2 27.4 %all-gather.9.cloned.1.call-done = bf16[1536,3072]{1,0:T(8,128)(2,1)} async-done(((bf16[96,3072]{1,0:T(8,128)(2,1)}), bf16[1536,3072]{1,0:T(8,128)(2,1)}) %all-gather.9.cloned.1.call-update) | async-done | bytes 9437200 | tf_op jit(solution)/shard_map/all_gather | solution.py:145
  378.6 12.4 %convolution_convert_fusion = bf16[256,1536]{1,0:T(8,128)(2,1)} fusion(bf16[3072,1536]{1,0:T(8,128)(2,1)} %all-gather.11.cloned.1.call-done, bf16[256,1536]{1,0:T(8,128)(2,1)S(1)} %convolution_convert_fusion.1, bf16[1536,3072]{1,0:T(8,128)(2,1)} %all-gather.9.cloned.1.call-done), kind=kOutput, calls=%fused_computation.28 | convolution fusion | flops 4839309312 | bytes 20447232 | tf_op jit(solution)/shard_map/dot_general | solution.py:150
  (128 shorter events, 73.4 us)
Async XLA Ops:
  7.2 343.2 %copy-start = (bf16[768,1536]{1,0:T(8,128)(2,1)S(1)}, bf16[768,1536]{1,0:T(8,128)(2,1)}, u32[]{:S(2)}) copy-start(bf16[768,1536]{1,0:T(8,128)(2,1)} %param.15) | copy-start | bytes 7077892
  7.2 308.7 %all-gather.13.cloned.1.call-start = ((), (), s32[]{:S(2)}) async-start(), calls=%async_computation.2 | async-start | bytes 6684672 | tf_op jit(solution)/shard_map/all_gather | solution.py:35
  9.2 79.7 %copy-start.11 = (s32[64]{0:T(128)}, s32[64]{0:T(128)S(1)}, u32[]{:S(2)}) copy-start(s32[64]{0:T(128)S(1)} %broadcast_subtract_fusion) | copy-start | bytes 772
  15.0 80.0 %copy-start.1 = (bf16[256,768]{1,0:T(8,128)(2,1)S(1)}, bf16[256,768]{1,0:T(8,128)(2,1)}, u32[]{:S(2)}) copy-start(bf16[256,768]{1,0:T(8,128)(2,1)} %param.11) | copy-start | bytes 1179652
  15.0 80.0 %copy-start.2 = (bf16[256,768]{1,0:T(8,128)(2,1)S(1)}, bf16[256,768]{1,0:T(8,128)(2,1)}, u32[]{:S(2)}) copy-start(bf16[256,768]{1,0:T(8,128)(2,1)} %param.12) | copy-start | bytes 1179652
  88.9 7.0 %copy-start.17 = (s32[12]{0:T(128)S(1)}, s32[12]{0:T(128)}, u32[]{:S(2)}) copy-start(s32[12]{0:T(128)} %param.13) | copy-start | bytes 148
  90.2 0.9 copy-start.3
  93.5 257.7 %all-gather.11.cloned.1.call-start = ((), (), s32[]{:S(2)}) async-start(), calls=%async_computation.1 | async-start | bytes 10027008 | tf_op jit(solution)/shard_map/all_gather | solution.py:152
  94.2 284.4 %all-gather.9.cloned.1.call-start = ((), (), s32[]{:S(2)}) async-start(), calls=%async_computation | async-start | bytes 10027008 | tf_op jit(solution)/shard_map/all_gather | solution.py:145
  95.9 21.7 %collective-permute-start.2 = (bf16[2,256,768]{2,1,0:T(8,128)(2,1)}, bf16[2,256,768]{2,1,0:T(8,128)(2,1)}, u32[]{:S(2)}, u32[]{:S(2)}) collective-permute-start(bf16[2,256,768]{2,1,0:T(8,128)(2,1)} %pad_maximum_fusion.9), channel_id=1, source_target_pairs={{0,15},{1,0},{2,1},{3,2},{4,3},{5,4},{6,5},{7,6},{8,7},{9,8},{10,9... | collective-permute-start | bytes 2359304 | tf_op jit(solution)/shard_map/ppermute | solution.py:31
  97.1 0.6 copy-start.15
  119.8 19.0 %collective-permute-start.3 = (bf16[2,256,768]{2,1,0:T(8,128)(2,1)}, bf16[2,256,768]{2,1,0:T(8,128)(2,1)}, u32[]{:S(2)}, u32[]{:S(2)}) collective-permute-start(bf16[2,256,768]{2,1,0:T(8,128)(2,1)} %broadcast_select_fusion), channel_id=1, source_target_pairs={{0,14},{1,15},{2,0},{3,1},{4,2},{5,3},{6,4},{7,5},{8,6},{9,7},{10,... | collective-permute-start | bytes 2359304 | tf_op jit(solution)/shard_map/ppermute | solution.py:31
  121.1 45.5 %copy-start.14 = (pred[12]{0:T(512)(128)(4,1)S(1)}, pred[12]{0:T(512)(128)(4,1)}, u32[]{:S(2)}) copy-start(pred[12]{0:T(512)(128)(4,1)} %get-tuple-element.211) | copy-start | bytes 40
  141.1 78.4 %collective-permute-start.4 = (bf16[2,256,768]{2,1,0:T(8,128)(2,1)}, bf16[2,256,768]{2,1,0:T(8,128)(2,1)}, u32[]{:S(2)}, u32[]{:S(2)}) collective-permute-start(bf16[2,256,768]{2,1,0:T(8,128)(2,1)} %broadcast_select_fusion.1), channel_id=1, source_target_pairs={{0,12},{1,13},{2,14},{3,15},{4,0},{5,1},{6,2},{7,3},{8,4},{9,5},{1... | collective-permute-start | bytes 2359304 | tf_op jit(solution)/shard_map/ppermute | solution.py:31
  142.1 80.4 %collective-permute-start = (bf16[2,128,768]{2,1,0:T(8,128)(2,1)}, bf16[2,128,768]{2,1,0:T(8,128)(2,1)}, u32[]{:S(2)}, u32[]{:S(2)}) collective-permute-start(bf16[2,128,768]{2,1,0:T(8,128)(2,1)} %get-tuple-element.209), channel_id=1, source_target_pairs={{0,1},{1,2},{2,3},{3,4},{4,5},{5,6},{6,7},{7,8},{8,9},{9,10},{10,1... | collective-permute-start | bytes 1179656 | tf_op jit(solution)/shard_map/ppermute | solution.py:19
  157.4 61.5 %copy-start.12 = (s32[64]{0:T(128)S(1)}, s32[64]{0:T(128)}, u32[]{:S(2)}) copy-start(s32[64]{0:T(128)} %copy-done.11) | copy-start | bytes 772
  157.4 65.1 %collective-permute-start.1 = (bf16[2,128,768]{2,1,0:T(8,128)(2,1)}, bf16[2,128,768]{2,1,0:T(8,128)(2,1)}, u32[]{:S(2)}, u32[]{:S(2)}) collective-permute-start(bf16[2,128,768]{2,1,0:T(8,128)(2,1)} %get-tuple-element.210), channel_id=1, source_target_pairs={{1,0},{2,1},{3,2},{4,3},{5,4},{6,5},{7,6},{8,7},{9,8},{10,9},{11,1... | collective-permute-start | bytes 1179656 | tf_op jit(solution)/shard_map/ppermute | solution.py:21
  200.6 18.4 %copy-start.9 = (f32[16,12,64]{2,1,0:T(8,128)}, f32[16,12,64]{2,1,0:T(8,128)S(1)}, u32[]{:S(2)}) copy-start(f32[16,12,64]{2,1,0:T(8,128)S(1)} %all-gather.4) | copy-start | bytes 147460
  218.8 0.7 copy-start.10
  221.9 71.4 %collective-permute-start.5 = (bf16[2,256,768]{2,1,0:T(8,128)(2,1)}, bf16[2,256,768]{2,1,0:T(8,128)(2,1)}, u32[]{:S(2)}, u32[]{:S(2)}) collective-permute-start(bf16[2,256,768]{2,1,0:T(8,128)(2,1)} %broadcast_select_fusion.2), channel_id=1, source_target_pairs={{0,8},{1,9},{2,10},{3,11},{4,12},{5,13},{6,14},{7,15},{8,0},{9,1},... | collective-permute-start | bytes 2359304 | tf_op jit(solution)/shard_map/ppermute | solution.py:31
  298.3 2.6 copy-start.4
  298.3 2.6 copy-start.5
  301.6 1.9 copy-start.7
  301.6 2.0 copy-start.8
  303.6 7.2 %copy-start.6 = (bf16[64,768]{0,1:T(8,128)(2,1)S(1)}, bf16[64,768]{0,1:T(8,128)(2,1)}, u32[]{:S(2)}) copy-start(bf16[64,768]{0,1:T(8,128)(2,1)} %copy.93) | copy-start | bytes 294916
  316.9 32.8 %copy-start.13 = (s32[64]{0:T(128)S(1)}, s32[64]{0:T(128)}, u32[]{:S(2)}) copy-start(s32[64]{0:T(128)} %copy-done.11) | copy-start | bytes 772
  316.9 32.8 %copy-start.16 = (pred[256]{0:T(512)(128)(4,1)S(1)}, pred[256]{0:T(512)(128)(4,1)}, u32[]{:S(2)}) copy-start(pred[256]{0:T(512)(128)(4,1)} %broadcast_compare_fusion) | copy-start | bytes 772
  351.1 39.9 %copy-start.18 = (bf16[256,1536]{1,0:T(8,128)(2,1)}, bf16[256,1536]{1,0:T(8,128)(2,1)S(1)}, u32[]{:S(2)}) copy-start(bf16[256,1536]{1,0:T(8,128)(2,1)S(1)} %convolution_convert_fusion.1) | copy-start | bytes 2359300
Sparse Core Ops, SparseCore 0:
  93.6 83.7 all-gather.12
  179.7 116.0 all-gather.10
  298.1 80.4 all-gather.8
where the time goes:
time: 400 us; the launch traced here: 398 us
  blocking collectives  112 us (28%)
  waiting for transfers between devices  106 us (26%)
  local copies, waits for them, and re-layouts  60.1 us (15%)
  other arithmetic  50.4 us (13%)
  matrix products  34.8 us (9%)
  starting transfers between devices  19.9 us (5%)
  between operations  14.1 us (4%)
    ppermute x4, waiting for transfers between devices, passed_along(): return lax.ppermute(value, axis, pairs)  77.1 us
    psum x1, blocking collectives, per_device(): glob_q, glob_k, glob_v = lax.psum((picked[0], picked[1], picked[2]), 'seq')  70.1 us
    all_gather x2, blocking collectives, merged_2(): gathered = jax.tree.map(lambda a: lax.all_gather(a, axis), part)  41.9 us
    all_gather x1, waiting for transfers between devices, per_device(): lax.all_gather(mlp_up, 'seq', axis=0, tiled=True)  27.4 us
    add x15, other arithmetic, join_partials(): numer_first * scale_first[:, :, None]  20.8 us
    ppermute x1, starting transfers between devices, with_halo(): lax.ppermute(tail, axis, [(i, (i + 1) % count) for i in range(count)])  15.3 us
    dot_general x1, matrix products, per_device(): jnp.dot(columns, lax.all_gather(mlp_down, 'seq', axis=0, tiled=True), pre...  12.4 us
    add x15, other arithmetic, join_partials(): total_first * scale_first + total_second * scale_second  11 us
  transfers between devices with their start and end apart: 9, of which 4 were waited for; matrix products, arithmetic and copies ran while one was open for 29% of the time, Pallas kernels for 0%

commit v1 on v0

--- a/solution.py
+++ b/solution.py
@@ -7,6 +7,22 @@
 DH = 64
 BLK = 128
 GLOBALS = 64
+
+
+def gather_around(x, axis, dim):
+    ways, here, step = (lax.axis_size(axis), lax.axis_index(axis), x.shape[dim])
+    shape = [n * ways if d == dim else n for d, n in enumerate(x.shape)]
+    full = lax.dynamic_update_slice_in_dim(jnp.zeros(shape, x.dtype), x, here * step, axis=dim)
+    going_up = going_down = x
+    for far in range(1, ways // 2 + 1):
+        going_up = lax.ppermute(going_up, axis, [(d, (d + 1) % ways) for d in range(ways)])
+        full = lax.dynamic_update_slice_in_dim(full, going_up, (here - far) % ways * step, axis=dim)
+        if 2 * far < ways:
+            going_down = lax.ppermute(going_down, axis, [(d, (d - 1) % ways) for d in range(ways)])
+            full = lax.dynamic_update_slice_in_dim(
+                full, going_down, (here + far) % ways * step, axis=dim
+            )
+    return full
 
 
 def with_halo(cells, sides, width):
@@ -140,11 +156,7 @@
         jnp.bfloat16
     )
     columns = attended
-    pre_act = jnp.dot(
-        columns,
-        lax.all_gather(mlp_up, "seq", axis=0, tiled=True),
-        preferred_element_type=jnp.float32,
-    )
+    pre_act = jnp.dot(columns, gather_around(mlp_up, "seq", 0), preferred_element_type=jnp.float32)
     hidden = jax.nn.gelu(pre_act, approximate=True).astype(jnp.bfloat16)
     columns = hidden
     mlp_out = jnp.dot(

time: 400 us -> 454 us (1.14)
  the two profiles are of different devices: /device:TPU:0 before, /device:TPU:1 now
where the time goes in v1:
time: 454 us; the launch traced here: 451 us
  blocking collectives  125 us (28%)
  local copies, waits for them, and re-layouts  90.3 us (20%)
  starting transfers between devices  69.7 us (15%)
  waiting for transfers between devices  61.9 us (14%)
  other arithmetic  53.2 us (12%)
  matrix products  35.6 us (8%)
  between operations  14.6 us (3%)
    psum x1, blocking collectives, per_device(): glob_q, glob_k, glob_v = lax.psum((picked[0], picked[1], picked[2]), 'seq')  64.9 us
    all_gather x2, blocking collectives, merged_2(): gathered = jax.tree.map(lambda a: lax.all_gather(a, axis), part)  60.2 us
    ppermute x8, starting transfers between devices, gather_around(): lax.ppermute(going_up, axis, [(d, (d + 1) % ways) for d in range(ways)])  57.8 us
    ppermute x8, waiting for transfers between devices, gather_around(): lax.ppermute(going_up, axis, [(d, (d + 1) % ways) for d in range(ways)])  37.5 us
    add x15, other arithmetic, join_partials(): numer_first * scale_first[:, :, None]  20.7 us
    dynamic_update_slice x8, local copies, waits for them, and re-layouts, gather_around(): lax.dynamic_update_slice_in_dim(full, going_up, (here - far) % ways * ste...  13.4 us
    ppermute x4, waiting for transfers between devices, passed_along(): return lax.ppermute(value, axis, pairs)  13.3 us
    dot_general x1, matrix products, per_device(): jnp.dot(columns, lax.all_gather(mlp_down, 'seq', axis=0, tiled=True), pre...  12.7 us
  transfers between devices with their start and end apart: 23, of which 7 were waited for; matrix products, arithmetic and copies ran while one was open for 33% of the time, Pallas kernels for 0%

profile of v1, /device:TPU:1, one launch (start us, length us, event | category | flops | bytes accessed | tf_op | source)
XLA Modules:
  0.0 450.8 jit_solution(5572688236832103760)
XLA Ops:
  16.9 64.9 %all-reduce.2 = (bf16[64,768]{1,0:T(8,128)(2,1)}, bf16[64,768]{1,0:T(8,128)(2,1)}, bf16[64,768]{1,0:T(8,128)(2,1)}) all-reduce(f32[64,768]{1,0:T(8,128)} %fusion.47, f32[64,768]{1,0:T(8,128)} %fusion.48, f32[64,768]{1,0:T(8,128)} %fusion.49), channel_id=1, replica_groups=mesh['group'=2,'seq'=16] {'seq'}, use_global_device_ids=true, to_apply=%region_7.8 | all-reduce | flops 147456 | bytes 884736 | tf_op jit(solution)/shard_map/psum | solution.py:124
  89.9 3.7 collective-permute-start.7
  94.6 4.4 collective-permute-start.2
  108.1 40.5 %all-gather.4 = f32[16,12,64]{2,1,0:T(8,128)} all-gather(f32[1,12,64]{2,1,0:T(8,128)S(1)} %bitcast.103), channel_id=3, replica_groups=mesh['group'=2,'seq'=16] {'seq'}, dimensions={0}, use_global_device_ids=true | all-gather | bytes 52224 | tf_op jit(solution)/shard_map/all_gather | solution.py:51
  148.6 19.6 %all-gather.3 = f32[16,12,64]{2,1,0:T(8,128)} all-gather(f32[1,12,64]{2,1,0:T(8,128)S(1)} %bitcast.102), channel_id=2, replica_groups=mesh['group'=2,'seq'=16] {'seq'}, dimensions={0}, use_global_device_ids=true | all-gather | bytes 52224 | tf_op jit(solution)/shard_map/all_gather | solution.py:51
  180.3 4.8 %broadcast_in_dim.101 = bf16[1536,3072]{1,0:T(8,128)(2,1)} broadcast(bf16[]{:T(256)} %constant.174.clone.1), dimensions={} | broadcast | bytes 9437186 | tf_op jit(solution)/shard_map/broadcast_in_dim | solution.py:15
  188.5 2.4 pad_maximum_fusion.2
  190.9 2.6 copy.71
  193.5 3.5 reshape.91
  197.0 5.1 %fusion.65 = (bf16[2,2,128,12,64]{2,1,4,3,0:T(2,128)(2,1)S(1)}, bf16[2,2,128,12,64]{2,1,4,3,0:T(2,128)(2,1)S(1)}, bf16[2,2,128,12,64]{2,1,4,3,0:T(2,128)(2,1)S(1)}) fusion(bf16[2,4,128,12,64]{2,1,4,3,0:T(4,128)(2,1)} %reshape.91), kind=kLoop, calls=%fused_computation.114 | loop fusion | bytes 4718592 | tf_op jit(solution)/shard_map/slice | solution.py:130
  209.1 2.6 collective-permute-start.3
  217.8 2.7 reshape.95
  220.6 13.3 %collective-permute-done.8 = bf16[96,3072]{1,0:T(8,128)(2,1)} collective-permute-done((bf16[96,3072]{1,0:T(8,128)(2,1)}, bf16[96,3072]{1,0:T(8,128)(2,1)}, u32[]{:S(2)}, u32[]{:S(2)}) %collective-permute-start.8) | collective-permute-done | bytes 589856 | tf_op jit(solution)/shard_map/ppermute | solution.py:18
  233.9 2.6 collective-permute-start.10
  236.4 11.1 %collective-permute-done.9 = bf16[96,3072]{1,0:T(8,128)(2,1)} collective-permute-done((bf16[96,3072]{1,0:T(8,128)(2,1)}, bf16[96,3072]{1,0:T(8,128)(2,1)}, u32[]{:S(2)}, u32[]{:S(2)}) %collective-permute-start.9) | collective-permute-done | bytes 589856 | tf_op jit(solution)/shard_map/ppermute | solution.py:21
  249.4 8.2 %collective-permute-done.3 = bf16[2,256,768]{2,1,0:T(8,128)(2,1)} collective-permute-done((bf16[2,256,768]{2,1,0:T(8,128)(2,1)}, bf16[2,256,768]{2,1,0:T(8,128)(2,1)}, u32[]{:S(2)}, u32[]{:S(2)}) %collective-permute-start.3) | collective-permute-done | bytes 786464 | tf_op jit(solution)/shard_map/ppermute | solution.py:47
  257.6 2.4 broadcast_select_fusion.1
  264.4 10.2 %collective-permute-done.10 = bf16[96,3072]{1,0:T(8,128)(2,1)} collective-permute-done((bf16[96,3072]{1,0:T(8,128)(2,1)}, bf16[96,3072]{1,0:T(8,128)(2,1)}, u32[]{:S(2)}, u32[]{:S(2)}) %collective-permute-start.10) | collective-permute-done | bytes 589856 | tf_op jit(solution)/shard_map/ppermute | solution.py:18
  274.6 2.5 collective-permute-start.12
  281.5 5.1 %collective-permute-done.4 = bf16[2,256,768]{2,1,0:T(8,128)(2,1)} collective-permute-done((bf16[2,256,768]{2,1,0:T(8,128)(2,1)}, bf16[2,256,768]{2,1,0:T(8,128)(2,1)}, u32[]{:S(2)}, u32[]{:S(2)}) %collective-permute-start.4) | collective-permute-done | bytes 786464 | tf_op jit(solution)/shard_map/ppermute | solution.py:47
  289.0 34.6 %collective-permute-start.14 = (bf16[96,3072]{1,0:T(8,128)(2,1)}, bf16[96,3072]{1,0:T(8,128)(2,1)}, u32[]{:S(2)}, u32[]{:S(2)}) collective-permute-start(bf16[96,3072]{1,0:T(8,128)(2,1)} %collective-permute-done.12), channel_id=1, source_target_pairs={{0,1},{1,2},{2,3},{3,4},{4,5},{5,6},{6,7},{7,8},{8,9},{9,10},{10,1... | collective-permute-start | bytes 1769480 | tf_op jit(solution)/shard_map/ppermute | solution.py:18
  329.8 2.8 reshape.93
  340.4 2.7 reshape.92
  343.1 2.5 fusion.36
  349.2 7.1 %fusion.66 = (f32[2,12,128]{2,1,0:T(8,128)S(1)}, f32[2,12,128,576]{2,3,1,0:T(8,128)}) fusion(bf16[2,64,12,64]{1,3,2,0:T(8,128)(2,1)S(1)} %broadcast_in_dim.100, bf16[2,512,12,64]{1,3,2,0:T(8,128)(2,1)} %get-tuple-element.205, bf16[2,128,12,64]{1,0,3,2:T(2,128)(2,1)S(1)} %copy-done.8), kind=kOutput, calls=%fused_computation.115 | convolution fusion | flops 235340352 | bytes 9252864 | tf_op jit(solution)/shard_map/sub | solution.py:73
  356.4 4.3 fusion.30
  361.4 11.1 %collective-permute-start.18 = (bf16[96,3072]{1,0:T(8,128)(2,1)}, bf16[96,3072]{1,0:T(8,128)(2,1)S(1)}, u32[]{:S(2)}, u32[]{:S(2)}) collective-permute-start(bf16[96,3072]{1,0:T(8,128)(2,1)} %collective-permute-done.16), channel_id=1, source_target_pairs={{0,1},{1,2},{2,3},{3,4},{4,5},{5,6},{6,7},{7,8},{8,9},{9,10},{10,1... | collective-permute-start | bytes 1769480 | tf_op jit(solution)/shard_map/ppermute | solution.py:18
  376.3 8.9 %collective-permute-done.18 = bf16[96,3072]{1,0:T(8,128)(2,1)S(1)} collective-permute-done((bf16[96,3072]{1,0:T(8,128)(2,1)}, bf16[96,3072]{1,0:T(8,128)(2,1)S(1)}, u32[]{:S(2)}, u32[]{:S(2)}) %collective-permute-start.18) | collective-permute-done | bytes 589856 | tf_op jit(solution)/shard_map/ppermute | solution.py:18
  385.3 2.4 collective-permute-start.20
  389.4 5.1 %collective-permute-done.20 = bf16[96,3072]{1,0:T(8,128)(2,1)S(1)} collective-permute-done((bf16[96,3072]{1,0:T(8,128)(2,1)S(1)}, bf16[96,3072]{1,0:T(8,128)(2,1)S(1)}, u32[]{:S(2)}, u32[]{:S(2)}) %collective-permute-start.20) | collective-permute-done | bytes 589856 | tf_op jit(solution)/shard_map/ppermute | solution.py:18
  396.4 32.1 %while.19 = (s32[]{:T(128)}, f32[12,64]{1,0:T(8,128)S(1)}, f32[12,64]{1,0:T(8,128)S(1)}, f32[12,64,64]{2,1,0:T(8,128)S(1)}, f32[16,12,64]{2,1,0:T(8,128)}, /*ind...) while((s32[]{:T(128)}, f32[12,64]{1,0:T(8,128)S(1)}, ...), condition=%wide.region_5.6_spmd, body=%wide.region_4.5_spmd.sunk | while | flops 152069 | bytes 620695 | solution.py:56
  431.3 12.7 %convolution_convert_fusion = bf16[256,1536]{1,0:T(8,128)(2,1)} fusion(bf16[3072,1536]{1,0:T(8,128)(2,1)} %all-gather.8.cloned.1.call-done, bf16[256,1536]{1,0:T(8,128)(2,1)} %convolution_convert_fusion.1, bf16[1536,3072]{1,0:T(8,128)(2,1)} %constant_dynamic-update-slice_fusion), kind=kOutput, calls=%fused_computation.28 | convolution fusion | flops 4839309312 | bytes 20447232 | tf_op jit(solution)/shard_map/dot_general | solution.py:162
  (166 shorter events, 129.5 us)
Async XLA Ops:
  7.2 422.5 %copy-start = (bf16[768,1536]{1,0:T(8,128)(2,1)S(1)}, bf16[768,1536]{1,0:T(8,128)(2,1)}, u32[]{:S(2)}) copy-start(bf16[768,1536]{1,0:T(8,128)(2,1)} %param.15) | copy-start | bytes 7077892
  7.2 86.4 %copy-start.1 = (bf16[256,768]{1,0:T(8,128)(2,1)S(1)}, bf16[256,768]{1,0:T(8,128)(2,1)}, u32[]{:S(2)}) copy-start(bf16[256,768]{1,0:T(8,128)(2,1)} %param.11) | copy-start | bytes 1179652
  7.2 86.4 %copy-start.2 = (bf16[256,768]{1,0:T(8,128)(2,1)S(1)}, bf16[256,768]{1,0:T(8,128)(2,1)}, u32[]{:S(2)}) copy-start(bf16[256,768]{1,0:T(8,128)(2,1)} %param.12) | copy-start | bytes 1179652
  7.2 388.1 %all-gather.10.cloned.1.call-start = ((), (), s32[]{:S(2)}) async-start(), calls=%async_computation.1 | async-start | bytes 6684672 | tf_op jit(solution)/shard_map/all_gather | solution.py:51
  9.2 74.4 %copy-start.10 = (s32[64]{0:T(128)}, s32[64]{0:T(128)S(1)}, u32[]{:S(2)}) copy-start(s32[64]{0:T(128)S(1)} %broadcast_subtract_fusion) | copy-start | bytes 772
  88.2 343.1 %all-gather.8.cloned.1.call-start = ((), (), s32[]{:S(2)}) async-start(), calls=%async_computation | async-start | bytes 10027008 | tf_op jit(solution)/shard_map/all_gather | solution.py:164
  88.2 117.2 %collective-permute-start.6 = (bf16[96,3072]{1,0:T(8,128)(2,1)}, bf16[96,3072]{1,0:T(8,128)(2,1)}, u32[]{:S(2)}, u32[]{:S(2)}) collective-permute-start(bf16[96,3072]{1,0:T(8,128)(2,1)} %param.16), channel_id=1, source_target_pairs={{0,1},{1,2},{2,3},{3,4},{4,5},{5,6},{6,7},{7,8},{8,9},{9,10},{10,1... | collective-permute-start | bytes 1769480 | tf_op jit(solution)/shard_map/ppermute | solution.py:18
  89.9 116.8 %collective-permute-start.7 = (bf16[96,3072]{1,0:T(8,128)(2,1)}, bf16[96,3072]{1,0:T(8,128)(2,1)}, u32[]{:S(2)}, u32[]{:S(2)}) collective-permute-start(bf16[96,3072]{1,0:T(8,128)(2,1)} %param.16), channel_id=1, source_target_pairs={{0,15},{1,0},{2,1},{3,2},{4,3},{5,4},{6,5},{7,6},{8,7},{9,8},{10,9... | collective-permute-start | bytes 1769480 | tf_op jit(solution)/shard_map/ppermute | solution.py:21
  94.6 112.2 %collective-permute-start.2 = (bf16[2,256,768]{2,1,0:T(8,128)(2,1)}, bf16[2,256,768]{2,1,0:T(8,128)(2,1)}, u32[]{:S(2)}, u32[]{:S(2)}) collective-permute-start(bf16[2,256,768]{2,1,0:T(8,128)(2,1)} %pad_maximum_fusion.9), channel_id=1, source_target_pairs={{0,15},{1,0},{2,1},{3,2},{4,3},{5,4},{6,5},{7,6},{8,7},{9,8},{10,9... | collective-permute-start | bytes 2359304 | tf_op jit(solution)/shard_map/ppermute | solution.py:47
  99.9 88.6 %collective-permute-start = (bf16[2,128,768]{2,1,0:T(8,128)(2,1)}, bf16[2,128,768]{2,1,0:T(8,128)(2,1)}, u32[]{:S(2)}, u32[]{:S(2)}) collective-permute-start(bf16[2,128,768]{2,1,0:T(8,128)(2,1)} %get-tuple-element.209), channel_id=1, source_target_pairs={{0,1},{1,2},{2,3},{3,4},{4,5},{5,6},{6,7},{7,8},{8,9},{9,10},{10,1... | collective-permute-start | bytes 1179656 | tf_op jit(solution)/shard_map/ppermute | solution.py:35
  99.9 88.6 %collective-permute-start.1 = (bf16[2,128,768]{2,1,0:T(8,128)(2,1)}, bf16[2,128,768]{2,1,0:T(8,128)(2,1)}, u32[]{:S(2)}, u32[]{:S(2)}) collective-permute-start(bf16[2,128,768]{2,1,0:T(8,128)(2,1)} %get-tuple-element.210), channel_id=1, source_target_pairs={{1,0},{2,1},{3,2},{4,3},{5,4},{6,5},{7,6},{8,7},{9,8},{10,9},{11,1... | collective-permute-start | bytes 1179656 | tf_op jit(solution)/shard_map/ppermute | solution.py:37
  197.0 9.7 %copy-start.9 = (pred[768]{0:T(1024)(128)(4,1)S(1)}, pred[768]{0:T(1024)(128)(4,1)}, u32[]{:S(2)}) copy-start(pred[768]{0:T(1024)(128)(4,1)} %broadcast_in_dim.92) | copy-start | bytes 2308
  205.4 28.4 %collective-permute-start.8 = (bf16[96,3072]{1,0:T(8,128)(2,1)}, bf16[96,3072]{1,0:T(8,128)(2,1)}, u32[]{:S(2)}, u32[]{:S(2)}) collective-permute-start(bf16[96,3072]{1,0:T(8,128)(2,1)} %collective-permute-done.6), channel_id=1, source_target_pairs={{0,1},{1,2},{2,3},{3,4},{4,5},{5,6},{6,7},{7,8},{8,9},{9,10},{10,1... | collective-permute-start | bytes 1769480 | tf_op jit(solution)/shard_map/ppermute | solution.py:18
  206.7 40.8 %collective-permute-start.9 = (bf16[96,3072]{1,0:T(8,128)(2,1)}, bf16[96,3072]{1,0:T(8,128)(2,1)}, u32[]{:S(2)}, u32[]{:S(2)}) collective-permute-start(bf16[96,3072]{1,0:T(8,128)(2,1)} %collective-permute-done.7), channel_id=1, source_target_pairs={{0,15},{1,0},{2,1},{3,2},{4,3},{5,4},{6,5},{7,6},{8,7},{9,8},{10,9... | collective-permute-start | bytes 1769480 | tf_op jit(solution)/shard_map/ppermute | solution.py:21
  209.1 48.5 %collective-permute-start.3 = (bf16[2,256,768]{2,1,0:T(8,128)(2,1)}, bf16[2,256,768]{2,1,0:T(8,128)(2,1)}, u32[]{:S(2)}, u32[]{:S(2)}) collective-permute-start(bf16[2,256,768]{2,1,0:T(8,128)(2,1)} %broadcast_select_fusion), channel_id=1, source_target_pairs={{0,14},{1,15},{2,0},{3,1},{4,2},{5,3},{6,4},{7,5},{8,6},{9,7},{10,... | collective-permute-start | bytes 2359304 | tf_op jit(solution)/shard_map/ppermute | solution.py:47
  233.9 40.7 %collective-permute-start.10 = (bf16[96,3072]{1,0:T(8,128)(2,1)}, bf16[96,3072]{1,0:T(8,128)(2,1)}, u32[]{:S(2)}, u32[]{:S(2)}) collective-permute-start(bf16[96,3072]{1,0:T(8,128)(2,1)} %collective-permute-done.8), channel_id=1, source_target_pairs={{0,1},{1,2},{2,3},{3,4},{4,5},{5,6},{6,7},{7,8},{8,9},{9,10},{10,1... | collective-permute-start | bytes 1769480 | tf_op jit(solution)/shard_map/ppermute | solution.py:18
  247.5 29.6 %collective-permute-start.11 = (bf16[96,3072]{1,0:T(8,128)(2,1)}, bf16[96,3072]{1,0:T(8,128)(2,1)}, u32[]{:S(2)}, u32[]{:S(2)}) collective-permute-start(bf16[96,3072]{1,0:T(8,128)(2,1)} %collective-permute-done.9), channel_id=1, source_target_pairs={{0,15},{1,0},{2,1},{3,2},{4,3},{5,4},{6,5},{7,6},{8,7},{9,8},{10,9... | collective-permute-start | bytes 1769480 | tf_op jit(solution)/shard_map/ppermute | solution.py:21
  260.0 26.6 %collective-permute-start.4 = (bf16[2,256,768]{2,1,0:T(8,128)(2,1)}, bf16[2,256,768]{2,1,0:T(8,128)(2,1)}, u32[]{:S(2)}, u32[]{:S(2)}) collective-permute-start(bf16[2,256,768]{2,1,0:T(8,128)(2,1)} %broadcast_select_fusion.1), channel_id=1, source_target_pairs={{0,12},{1,13},{2,14},{3,15},{4,0},{5,1},{6,2},{7,3},{8,4},{9,5},{1... | collective-permute-start | bytes 2359304 | tf_op jit(solution)/shard_map/ppermute | solution.py:47
  274.6 14.4 %collective-permute-start.12 = (bf16[96,3072]{1,0:T(8,128)(2,1)}, bf16[96,3072]{1,0:T(8,128)(2,1)}, u32[]{:S(2)}, u32[]{:S(2)}) collective-permute-start(bf16[96,3072]{1,0:T(8,128)(2,1)} %collective-permute-done.10), channel_id=1, source_target_pairs={{0,1},{1,2},{2,3},{3,4},{4,5},{5,6},{6,7},{7,8},{8,9},{9,10},{10,1... | collective-permute-start | bytes 1769480 | tf_op jit(solution)/shard_map/ppermute | solution.py:18
  277.1 46.5 %collective-permute-start.13 = (bf16[96,3072]{1,0:T(8,128)(2,1)}, bf16[96,3072]{1,0:T(8,128)(2,1)}, u32[]{:S(2)}, u32[]{:S(2)}) collective-permute-start(bf16[96,3072]{1,0:T(8,128)(2,1)} %collective-permute-done.11), channel_id=1, source_target_pairs={{0,15},{1,0},{2,1},{3,2},{4,3},{5,4},{6,5},{7,6},{8,7},{9,8},{10,9... | collective-permute-start | bytes 1769480 | tf_op jit(solution)/shard_map/ppermute | solution.py:21
  289.0 49.2 %collective-permute-start.5 = (bf16[2,256,768]{2,1,0:T(8,128)(2,1)}, bf16[2,256,768]{2,1,0:T(8,128)(2,1)}, u32[]{:S(2)}, u32[]{:S(2)}) collective-permute-start(bf16[2,256,768]{2,1,0:T(8,128)(2,1)} %broadcast_select_fusion.2), channel_id=1, source_target_pairs={{0,8},{1,9},{2,10},{3,11},{4,12},{5,13},{6,14},{7,15},{8,0},{9,1},... | collective-permute-start | bytes 2359304 | tf_op jit(solution)/shard_map/ppermute | solution.py:47
  289.0 43.6 %collective-permute-start.14 = (bf16[96,3072]{1,0:T(8,128)(2,1)}, bf16[96,3072]{1,0:T(8,128)(2,1)}, u32[]{:S(2)}, u32[]{:S(2)}) collective-permute-start(bf16[96,3072]{1,0:T(8,128)(2,1)} %collective-permute-done.12), channel_id=1, source_target_pairs={{0,1},{1,2},{2,3},{3,4},{4,5},{5,6},{6,7},{7,8},{8,9},{9,10},{10,1... | collective-permute-start | bytes 1769480 | tf_op jit(solution)/shard_map/ppermute | solution.py:18
  323.6 10.7 %collective-permute-start.15 = (bf16[96,3072]{1,0:T(8,128)(2,1)}, bf16[96,3072]{1,0:T(8,128)(2,1)}, u32[]{:S(2)}, u32[]{:S(2)}) collective-permute-start(bf16[96,3072]{1,0:T(8,128)(2,1)} %collective-permute-done.13), channel_id=1, source_target_pairs={{0,15},{1,0},{2,1},{3,2},{4,3},{5,4},{6,5},{7,6},{8,7},{9,8},{10,9... | collective-permute-start | bytes 1769480 | tf_op jit(solution)/shard_map/ppermute | solution.py:21
  329.8 15.8 %copy-start.4 = (bf16[2,2,128,12,64]{2,4,3,1,0:T(8,128)(2,1)S(1)}, bf16[2,2,128,12,64]{2,4,3,1,0:T(8,128)(2,1)}, u32[]{:S(2)}) copy-start(bf16[2,2,128,12,64]{2,4,3,1,0:T(8,128)(2,1)} %copy.95) | copy-start | bytes 2359300
  332.6 28.8 %collective-permute-start.16 = (bf16[96,3072]{1,0:T(8,128)(2,1)}, bf16[96,3072]{1,0:T(8,128)(2,1)}, u32[]{:S(2)}, u32[]{:S(2)}) collective-permute-start(bf16[96,3072]{1,0:T(8,128)(2,1)} %collective-permute-done.14), channel_id=1, source_target_pairs={{0,1},{1,2},{2,3},{3,4},{4,5},{5,6},{6,7},{7,8},{8,9},{9,10},{10,1... | collective-permute-start | bytes 1769480 | tf_op jit(solution)/shard_map/ppermute | solution.py:18
  334.3 38.2 %collective-permute-start.17 = (bf16[96,3072]{1,0:T(8,128)(2,1)}, bf16[96,3072]{1,0:T(8,128)(2,1)}, u32[]{:S(2)}, u32[]{:S(2)}) collective-permute-start(bf16[96,3072]{1,0:T(8,128)(2,1)} %collective-permute-done.15), channel_id=1, source_target_pairs={{0,15},{1,0},{2,1},{3,2},{4,3},{5,4},{6,5},{7,6},{8,7},{9,8},{10,9... | collective-permute-start | bytes 1769480 | tf_op jit(solution)/shard_map/ppermute | solution.py:21
  349.2 7.1 %copy-start.5 = (bf16[64,768]{0,1:T(8,128)(2,1)S(1)}, bf16[64,768]{0,1:T(8,128)(2,1)}, u32[]{:S(2)}) copy-start(bf16[64,768]{0,1:T(8,128)(2,1)} %copy.93) | copy-start | bytes 294916
  361.4 23.9 %collective-permute-start.18 = (bf16[96,3072]{1,0:T(8,128)(2,1)}, bf16[96,3072]{1,0:T(8,128)(2,1)S(1)}, u32[]{:S(2)}, u32[]{:S(2)}) collective-permute-start(bf16[96,3072]{1,0:T(8,128)(2,1)} %collective-permute-done.16), channel_id=1, source_target_pairs={{0,1},{1,2},{2,3},{3,4},{4,5},{5,6},{6,7},{7,8},{8,9},{9,10},{10,1... | collective-permute-start | bytes 1769480 | tf_op jit(solution)/shard_map/ppermute | solution.py:18
  372.5 16.1 %collective-permute-start.19 = (bf16[96,3072]{1,0:T(8,128)(2,1)}, bf16[96,3072]{1,0:T(8,128)(2,1)S(1)}, u32[]{:S(2)}, u32[]{:S(2)}) collective-permute-start(bf16[96,3072]{1,0:T(8,128)(2,1)} %collective-permute-done.17), channel_id=1, source_target_pairs={{0,15},{1,0},{2,1},{3,2},{4,3},{5,4},{6,5},{7,6},{8,7},{9,8},{10,9... | collective-permute-start | bytes 1769480 | tf_op jit(solution)/shard_map/ppermute | solution.py:21
  385.3 9.2 %collective-permute-start.20 = (bf16[96,3072]{1,0:T(8,128)(2,1)S(1)}, bf16[96,3072]{1,0:T(8,128)(2,1)S(1)}, u32[]{:S(2)}, u32[]{:S(2)}) collective-permute-start(bf16[96,3072]{1,0:T(8,128)(2,1)S(1)} %collective-permute-done.18), channel_id=1, source_target_pairs={{0,1},{1,2},{2,3},{3,4},{4,5},{5,6},{6,7},{7,8},{8,9},{9,10},{10,1... | collective-permute-start | bytes 1769480 | tf_op jit(solution)/shard_map/ppermute | solution.py:18
  388.5 40.5 %copy-start.11 = (s32[64]{0:T(128)S(1)}, s32[64]{0:T(128)}, u32[]{:S(2)}) copy-start(s32[64]{0:T(128)} %copy-done.10) | copy-start | bytes 772
  388.5 40.5 %copy-start.15 = (pred[256]{0:T(512)(128)(4,1)S(1)}, pred[256]{0:T(512)(128)(4,1)}, u32[]{:S(2)}) copy-start(pred[256]{0:T(512)(128)(4,1)} %broadcast_compare_fusion) | copy-start | bytes 772
  (7 other events, 17.4 us)
Sparse Core Ops, SparseCore 0:
  88.3 81.6 all-gather.9
  172.3 116.9 all-gather.7
